TPU v7x, 768 devices: a whole 4x8x12 slice. The times are simulated.
768 devices in a mesh: seq: 12 (over z_hi, x), head: 64 (over z_lo, y, core).
Axes of the slice: x: 4, y: 8, z: 12 (z_hi: 3, z_lo: 4; z = z_hi * 4 + z_lo), core: 2. Of those that a mesh axis runs over, the one named last changes fastest.
Arguments:
- query_rows: bfloat16 [24576, 64, 128], P('seq', 'head'), may hold values from -112 to 112
- key_rows: bfloat16 [24576, 64, 128], P('seq', 'head'), may hold values from -4 to 4
- value_rows: bfloat16 [24576, 64, 128], P('seq', 'head'), may hold values from -6 to 6
- attn_output: bfloat16 [24576, 64, 128], P('seq', 'head'), may hold values from -6 to 6
- out_grad: bfloat16 [24576, 4, 2048], P(('seq', 'head')), may hold values from -6 to 6
- neighbours: int32 [192, 4], replicated, may hold values from 0 to 191, as said below
- counts: int32 [192], replicated, may hold values from 2 to 128
Outputs:
- grad_query: bfloat16 [24576, 4, 2048], P(('seq', 'head'))
- grad_key: bfloat16 [24576, 4, 2048], P(('seq', 'head'))
- grad_value: bfloat16 [24576, 4, 2048], P(('seq', 'head'))
Inputs may be any that keep to these rules, and one draw needn't show every extreme that they name: `neighbours`: row t lists 4 different tiles, the first being t itself, each at most half of 16 tiles away from t.
All inputs are finite; a program needn't handle non-finite values.
Results may differ from a plain program's by a relative error of at most 0.011.
Values may be sent and summed in bfloat16 or wider, within the bound.
No kernel may reach another device: no remote copies, remote signals or barrier semaphores. Data moves between devices by JAX's collectives and lax.ppermute only.
A program may use at most 64 MiB of HBM per device.

v0:
```python
import math

import jax
import jax.numpy as jnp
from jax import lax
from jax.experimental import pallas as pl
from jax.experimental.pallas import tpu as pltpu
from jax.sharding import PartitionSpec as P

TILE = 128
NT = (((1,), (1,)), ((), ()))
NN = (((1,), (0,)), ((), ()))
TN = (((0,), (0,)), ((), ()))


def dot(a, b, dims):
    return lax.dot_general(a, b, dims, preferred_element_type=jnp.float32)


def span(t):
    return pl.ds(pl.multiple_of(t * TILE, TILE), TILE)


def start_copies(moves, sems):
    for i, (dst, choice) in enumerate(moves):
        if len(choice) == 1:
            pltpu.make_async_copy(choice[0], dst, sems.at[i]).start()
        else:
            far, use_far, near = choice

            @pl.when(use_far)
            def _():
                pltpu.make_async_copy(far, dst, sems.at[i]).start()

            @pl.when(jnp.logical_not(use_far))
            def _():
                pltpu.make_async_copy(near, dst, sems.at[i]).start()


def wait_copies(moves, sems):
    for i, (dst, choice) in enumerate(moves):
        pltpu.make_async_copy(choice[-1], dst, sems.at[i]).wait()


def stats_kernel(tiles_dev, nbr_count, ring_len):
    half_tiles = tiles_dev // 2
    half = half_tiles * TILE
    own = tiles_dev * TILE
    scale_two = TILE ** (-0.5) * math.log2(math.e)

    def kernel(
        shard, nbr, cnt, q_any, k_any, o_any, g_any, kv_lo, kv_hi, kz,
        stat_all, stat_lo, stat_hi,
        q, o, g, k_ext, sems,
    ):
        s = shard[0]
        first_tile = s * tiles_dev
        ext_base = first_tile - half_tiles
        col = lax.rem(s, ring_len)
        moves = (
            (k_ext.at[pl.ds(half, own)], (k_any,)),
            (q, (q_any,)),
            (o, (o_any,)),
            (g, (g_any,)),
            (k_ext.at[pl.ds(0, half)], (kz, col == 0, kv_lo.at[pl.ds(0, half)])),
            (
                k_ext.at[pl.ds(half + own, half)],
                (kz, col == ring_len - 1, kv_hi.at[pl.ds(0, half)]),
            ),
        )
        start_copies(moves, sems)
        wait_copies(moves, sems)
        rows = lax.broadcasted_iota(jnp.int32, (TILE, TILE), 0)

        def lse_of(t):
            tile = first_tile + t
            q_t = q[span(t), :]
            tops, totals = [], []
            for n in range(nbr_count):
                near = nbr[tile * nbr_count + n]
                score = dot(k_ext[span(near - ext_base), :], q_t, NT) * scale_two
                score = jnp.where(rows < cnt[near], score, -jnp.inf)
                peak = jnp.max(score, axis=0, keepdims=True)
                tops.append(peak)
                totals.append(jnp.sum(jnp.exp2(score - peak), axis=0, keepdims=True))
            top = tops[0]
            for peak in tops[1:]:
                top = jnp.maximum(top, peak)
            total = totals[0] * jnp.exp2(tops[0] - top)
            for part, peak in zip(totals[1:], tops[1:]):
                total = total + part * jnp.exp2(peak - top)
            g_t = jnp.where(rows < cnt[tile], g[span(t), :].astype(jnp.float32), 0.0)
            prod = g_t * o[span(t), :].astype(jnp.float32)
            delta = jnp.sum(prod.T, axis=0, keepdims=True)
            return top + jnp.log2(total), delta

        def step(i, carry):
            first = lse_of(2 * i)
            second = lse_of(2 * i + 1)
            for t, (log_row, delta) in ((2 * i, first), (2 * i + 1, second)):
                stat_all[pl.ds(t, 1), :] = log_row
                stat_all[pl.ds(tiles_dev + t, 1), :] = delta
            return carry

        lax.fori_loop(0, tiles_dev // 2, step, 0)
        for side, out in ((0, stat_lo), (1, stat_hi)):
            out[pl.ds(0, half_tiles), :] = stat_all[pl.ds(side * half_tiles, half_tiles), :]
            out[pl.ds(half_tiles, half_tiles), :] = stat_all[
                pl.ds(tiles_dev + side * half_tiles, half_tiles), :
            ]

    return kernel


def masked(ref, t, held):
    rows = lax.broadcasted_iota(jnp.int32, (TILE, TILE), 0)
    kept = jnp.where(rows < held, ref[span(t), :].astype(jnp.float32), 0.0)
    return kept.astype(jnp.bfloat16)


def pair_terms(key, value, held, q_t, g_t, log_row, delta):
    rows = lax.broadcasted_iota(jnp.int32, (TILE, TILE), 0)
    scale = TILE ** (-0.5)
    score = dot(key, q_t, NT) * (scale * math.log2(math.e))
    prob = jnp.exp2(jnp.where(rows < held, score - log_row, -jnp.inf))
    dprob = dot(value, g_t, NT)
    dscore = (prob * (dprob - delta) * scale).astype(jnp.bfloat16)
    return prob.astype(jnp.bfloat16), dscore


def own_kernel(tiles_dev, nbr_count, ring_len, peers):
    half_tiles = tiles_dev // 2
    half = half_tiles * TILE
    own = tiles_dev * TILE
    share = own // peers
    tile_peers = TILE // share

    def kernel(
        shard, nbr, cnt, q_any, k_any, v_any, g_any, kv_lo, kv_hi, kz, vz, stat_any,
        dq_ref, dk_ref, dv_ref, q, g, k_ext, v_ext, dk_acc, dv_acc, stats, sems,
    ):
        s = shard[0]
        first_tile = s * tiles_dev
        ext_base = first_tile - half_tiles
        col = lax.rem(s, ring_len)
        at_low = col == 0
        at_high = col == ring_len - 1
        first_half = pl.ds(0, half)
        second_half = pl.ds(half, half)
        above = pl.ds(half + own, half)
        moves = (
            (k_ext.at[pl.ds(half, own)], (k_any,)),
            (v_ext.at[pl.ds(half, own)], (v_any,)),
            (q, (q_any,)),
            (g, (g_any,)),
            (stats, (stat_any,)),
            (k_ext.at[first_half], (kz, at_low, kv_lo.at[first_half])),
            (k_ext.at[above], (kz, at_high, kv_hi.at[first_half])),
            (v_ext.at[first_half], (vz, at_low, kv_lo.at[second_half])),
            (v_ext.at[above], (vz, at_high, kv_hi.at[second_half])),
        )
        start_copies(moves, sems)
        zero = jnp.zeros((own, TILE), jnp.float32)
        dk_acc[pl.ds(0, own), :] = zero
        dv_acc[pl.ds(0, own), :] = zero
        wait_copies(moves, sems)

        def own_terms(t):
            tile = first_tile + t
            q_t = q[span(t), :]
            g_t = masked(g, t, cnt[tile])
            log_row = stats[pl.ds(t, 1), :]
            delta = stats[pl.ds(tiles_dev + t, 1), :]
            places, keys, probs, dscores = [], [], [], []
            for n in range(nbr_count):
                near = nbr[tile * nbr_count + n]
                place = near - ext_base
                mine = place - half_tiles
                places.append(jnp.where((mine >= 0) & (mine < tiles_dev), mine, tiles_dev))
                key = k_ext[span(place), :]
                prob, dscore = pair_terms(
                    key, v_ext[span(place), :], cnt[near], q_t, g_t, log_row, delta
                )
                keys.append(key)
                probs.append(prob)
                dscores.append(dscore)
            return t, q_t, g_t, places, keys, probs, dscores

        def own_sums(t, q_t, g_t, places, keys, probs, dscores):
            for mine, dscore, prob in zip(places, dscores, probs):
                dk_acc[span(mine), :] += dot(dscore, q_t, NN)
                dv_acc[span(mine), :] += dot(prob, g_t, NN)
            dq = dot(jnp.concatenate(dscores), jnp.concatenate(keys), TN)
            dq_ref[pl.ds(t * tile_peers, tile_peers)] = (
                dq.astype(jnp.bfloat16).reshape(tile_peers, share, TILE)
            )

        def own_step(i, carry):
            first = own_terms(2 * i)
            second = own_terms(2 * i + 1)
            own_sums(*first)
            own_sums(*second)
            return carry

        lax.fori_loop(0, tiles_dev // 2, own_step, 0)
        dk_ref[...] = dk_acc[pl.ds(0, own), :]
        dv_ref[...] = dv_acc[pl.ds(0, own), :]

    return kernel


def near_kernel(tiles_dev, tiles_all, nbr_count, ring_len, peers):
    half_tiles = tiles_dev // 2
    half = half_tiles * TILE
    own = tiles_dev * TILE
    share = own // peers

    def kernel(
        shard, nbr, cnt, k_any, v_any, kvq_lo, kvq_hi, qz, glo, ghi, gz, slo, shi, dq_any, dk_any, dv_any,
        joint, k, v, q_near, g_near, dk_acc, dv_acc, stats_near, pairs, sems,
    ):
        s = shard[0]
        first_tile = s * tiles_dev
        col = lax.rem(s, ring_len)
        at_low = col == 0
        at_high = col == ring_len - 1
        first_half = pl.ds(0, half)
        second_half = pl.ds(half, half)
        third_half = pl.ds(2 * half, half)
        moves = (
            (k, (k_any,)),
            (v, (v_any,)),
            (dk_acc.at[pl.ds(0, own)], (dk_any,)),
            (dv_acc.at[pl.ds(0, own)], (dv_any,)),
            (stats_near.at[0], (slo,)),
            (stats_near.at[1], (shi,)),
            (q_near.at[first_half], (qz, at_low, kvq_lo.at[third_half])),
            (q_near.at[second_half], (qz, at_high, kvq_hi.at[third_half])),
            (g_near.at[first_half], (gz, at_low, glo)),
            (g_near.at[second_half], (gz, at_high, ghi)),
            (joint.at[:, 0], (dq_any,)),
        )
        start_copies(moves, sems)

        def scan(i, count):
            tile = jnp.where(
                i < half_tiles, first_tile - half_tiles + i, first_tile + tiles_dev + i - half_tiles
            )
            inside = (tile >= 0) & (tile < tiles_all)
            safe = jnp.where(inside, tile, 0)
            for n in range(1, nbr_count):
                mine = nbr[safe * nbr_count + n] - first_tile
                hit = inside & (mine >= 0) & (mine < tiles_dev)
                pairs[0, count] = i
                pairs[1, count] = mine
                count = count + hit.astype(jnp.int32)
            return count

        count = lax.fori_loop(0, tiles_dev, scan, jnp.int32(0))
        pairs[0, count] = 0
        pairs[1, count] = tiles_dev
        wait_copies(moves, sems)

        def near_terms(index):
            i = pairs[0, index]
            mine = pairs[1, index]
            read = jnp.minimum(mine, tiles_dev - 1)
            side = jnp.where(i < half_tiles, 0, 1)
            line = i - side * half_tiles
            tile = first_tile + jnp.where(side == 0, i - half_tiles, tiles_dev + line)
            q_t = q_near[span(i), :]
            g_t = masked(g_near, i, cnt[jnp.clip(tile, 0, tiles_all - 1)])
            log_row = stats_near[side, pl.ds(line, 1), :]
            delta = stats_near[side, pl.ds(half_tiles + line, 1), :]
            held = cnt[first_tile + read]
            prob, dscore = pair_terms(k[span(read), :], v[span(read), :], held, q_t, g_t, log_row, delta)
            return mine, dot(dscore, q_t, NN), dot(prob, g_t, NN)

        def near_step(j, carry):
            first = near_terms(2 * j)
            second = near_terms(2 * j + 1)
            for mine, dk, dv in (first, second):
                dk_acc[span(mine), :] += dk
                dv_acc[span(mine), :] += dv
            return carry

        lax.fori_loop(0, (count + 1) // 2, near_step, 0)
        for which, acc in ((1, dk_acc), (2, dv_acc)):
            joint[:, which] = (
                acc[pl.ds(0, own), :].astype(jnp.bfloat16).reshape(peers, share, TILE)
            )

    return kernel


def routes(seq_count, ring_len):
    spots = [divmod(s, ring_len) for s in range(seq_count)]

    def pairs(move):
        out = []
        for s, (r, x) in enumerate(spots):
            to = move(r, x)
            if to is not None and 0 <= to[0] < seq_count // ring_len:
                out.append((s, to[0] * ring_len + to[1]))
        return out

    last = ring_len - 1

    def ends(at_first, at_last):
        return pairs(lambda r, x: at_first(r) if x == 0 else at_last(r) if x == last else None)

    return {
        "forward": [(i, i + 1) for i in range(seq_count - 1)],
        "backward": [(i + 1, i) for i in range(seq_count - 1)],
        "around": pairs(lambda r, x: (r, (x + 1) % ring_len)),
        "around_back": pairs(lambda r, x: (r, (x - 1) % ring_len)),
        "up": pairs(lambda r, x: (r, x + 1) if x < last else None),
        "down": pairs(lambda r, x: (r, x - 1) if x > 0 else None),
        "cross": ends(lambda r: (r - 1, last), lambda r: (r + 1, 0)),
        "far": ends(lambda r: (r + 1, 0), lambda r: (r - 1, last)),
        "inward": ends(lambda r: (r, 1), lambda r: (r, last - 1)),
        "inward_two": ends(lambda r: (r, last - 1), lambda r: (r, 1)),
        "outward_two": pairs(
            lambda r, x: (r + 1, 0) if x == 1 else (r - 1, last) if x == last - 1 else None
        ),
        "outward": pairs(
            lambda r, x: (r - 1, last) if x == 1 else (r + 1, 0) if x == last - 1 else None
        ),
    }


def device_work(query_rows, key_rows, value_rows, attn_output, out_grad, neighbours, counts):
    seq_rows, batch, width = out_grad.shape
    shard_tokens, _, head_dim = query_rows.shape
    nbr_count = neighbours.shape[1]
    tiles_all = counts.shape[0]
    tiles_dev = shard_tokens // TILE
    half = shard_tokens // 2
    peers = shard_tokens // seq_rows
    ring_len = 4
    route = routes(lax.axis_size("seq"), ring_len)
    shard = lax.axis_index("seq").astype(jnp.int32)
    at_start = lax.rem(shard, ring_len) == 0

    def move(rows, name):
        return lax.ppermute(rows, "seq", route[name])

    def edge(rows):
        return jnp.where(at_start, rows[:half], rows[half:])

    q = query_rows.reshape(shard_tokens, head_dim)
    k = key_rows.reshape(shard_tokens, head_dim)
    v = value_rows.reshape(shard_tokens, head_dim)
    o = attn_output.reshape(shard_tokens, head_dim)
    table = neighbours.reshape(-1)
    k_side = move(edge(k), "inward")
    v_side = move(edge(v), "inward_two")
    kvq_low = move(jnp.concatenate([k[half:], v[half:], q[half:]]), "around")
    kvq_high = move(jnp.concatenate([k[:half], v[:half], q[:half]]), "around_back")
    sent = out_grad.reshape(seq_rows, peers, head_dim).transpose(1, 0, 2)
    grads = lax.all_to_all(sent, "head", split_axis=0, concat_axis=0, tiled=True)
    grads = grads.reshape(shard_tokens, head_dim)
    k_far = move(k_side, "outward")
    v_far = move(v_side, "outward_two")
    q_low, q_high, grads = lax.optimization_barrier((kvq_low, kvq_high, grads))
    q_far = move(jnp.where(at_start, q_low[2 * half :], q_high[2 * half :]), "far")
    g_far = move(edge(grads), "cross")
    g_low = move(grads[half:], "up")
    g_high = move(grads[:half], "down")

    smem = pl.BlockSpec(memory_space=pltpu.SMEM)
    vmem = pl.BlockSpec(memory_space=pltpu.VMEM)
    hbm = pl.BlockSpec(memory_space=pl.ANY)
    stat = jax.ShapeDtypeStruct((tiles_dev, head_dim), jnp.float32)
    held = pltpu.VMEM((shard_tokens, head_dim), jnp.bfloat16)
    wide = pltpu.VMEM((2 * shard_tokens, head_dim), jnp.bfloat16)
    acc = pltpu.VMEM((shard_tokens + TILE, head_dim), jnp.float32)
    place = shard.reshape(1)
    stat_all, stat_low, stat_high = pl.pallas_call(
        stats_kernel(tiles_dev, nbr_count, ring_len),
        out_shape=(
            jax.ShapeDtypeStruct((2 * tiles_dev, head_dim), jnp.float32), stat, stat,
        ),
        in_specs=[smem] * 3 + [hbm] * 7,
        out_specs=(vmem,) * 3,
        scratch_shapes=[held, held, held, wide, pltpu.SemaphoreType.DMA((6,))],
        name="rowstats",
    )(place, table, counts, q, k, o, grads, kvq_low, kvq_high, k_far)
    near_low = move(stat_high, "forward")
    near_high = move(stat_low, "backward")
    sums = jax.ShapeDtypeStruct((shard_tokens, head_dim), jnp.float32)
    dq, dk, dv = pl.pallas_call(
        own_kernel(tiles_dev, nbr_count, ring_len, peers),
        out_shape=(
            jax.ShapeDtypeStruct((peers, seq_rows, head_dim), jnp.bfloat16), sums, sums,
        ),
        in_specs=[smem] * 3 + [hbm] * 9,
        out_specs=(vmem,) * 3,
        scratch_shapes=[
            held, held, wide, wide, acc, acc,
            pltpu.VMEM((2 * tiles_dev, head_dim), jnp.float32),
            pltpu.SemaphoreType.DMA((9,)),
        ],
        name="owngrads",
    )(place, table, counts, q, k, v, grads, kvq_low, kvq_high, k_far, v_far, stat_all)
    joint = pl.pallas_call(
        near_kernel(tiles_dev, tiles_all, nbr_count, ring_len, peers),
        out_shape=jax.ShapeDtypeStruct((peers, 3, seq_rows, head_dim), jnp.bfloat16),
        in_specs=[smem] * 3 + [hbm] * 13,
        out_specs=vmem,
        scratch_shapes=[
            held, held, held, held, acc, acc,
            pltpu.VMEM((2, tiles_dev, head_dim), jnp.float32),
            pltpu.SMEM((2, tiles_dev * nbr_count), jnp.int32),
            pltpu.SemaphoreType.DMA((11,)),
        ],
        name="neargrads",
    )(
        place, table, counts, k, v, kvq_low, kvq_high, q_far, g_low, g_high, g_far,
        near_low, near_high, dq, dk, dv,
    )
    back = lax.all_to_all(joint, "head", split_axis=0, concat_axis=0, tiled=True)

    def to_rows(block):
        return block.transpose(1, 0, 2).reshape(seq_rows, batch, width)

    return to_rows(back[:, 0]), to_rows(back[:, 1]), to_rows(back[:, 2])


def solution(mesh):
    placed = (
        P("seq", "head", None),
        P("seq", "head", None),
        P("seq", "head", None),
        P("seq", "head", None),
        P(("seq", "head"), None, None),
        P(),
        P(),
    )
    return jax.shard_map(
        device_work,
        mesh=mesh,
        in_specs=placed,
        out_specs=(
            P(("seq", "head"), None, None),
            P(("seq", "head"), None, None),
            P(("seq", "head"), None, None),
        ),
        check_vma=False,
    )
```

profile of v0, /device:TPU:259, one launch (start us, length us, event | category | flops | bytes accessed | tf_op | source)
XLA Modules:
  0.0 179.7 jit_solution(13539643185406865113)
XLA Ops:
  0.6 1.4 reshape.49
  2.1 1.1 copy.17
  3.2 13.6 %all-to-all-start = ((bf16[64,32,128]{2,1,0:T(8,128)(2,1)}), bf16[64,32,128]{2,1,0:T(8,128)(2,1)S(1)}, u32[]{:S(2)}, u32[]{:S(2)}) async-start(bf16[64,32,128]{2,1,0:T(8,128)(2,1)} %bitcast.40), calls=%async_computation | async-start | bytes 1048576 | tf_op jit(solution)/shard_map/all_to_all | solution.py:361
  17.0 1.0 pad_maximum_fusion
  18.0 3.1 %collective-permute-start = (bf16[3072,128]{1,0:T(8,128)(2,1)}, bf16[3072,128]{1,0:T(8,128)(2,1)S(1)}, u32[]{:S(2)}, u32[]{:S(2)}) collective-permute-start(bf16[3072,128]{1,0:T(8,128)(2,1)} %pad_maximum_fusion), channel_id=1, source_target_pairs={{0,64},{64,128},{128,192},{192,0},{256,320},{320,384},{384,448},{4... | collective-permute-start | bytes 2359304 | tf_op jit(solution)/shard_map/ppermute | solution.py:346
  21.1 1.0 pad_maximum_fusion.1
  22.0 2.2 %collective-permute-start.1 = (bf16[3072,128]{1,0:T(8,128)(2,1)}, bf16[3072,128]{1,0:T(8,128)(2,1)S(1)}, u32[]{:S(2)}, u32[]{:S(2)}) collective-permute-start(bf16[3072,128]{1,0:T(8,128)(2,1)} %pad_maximum_fusion.1), channel_id=1, source_target_pairs={{0,192},{64,0},{128,64},{192,128},{256,448},{320,256},{384,320},{4... | collective-permute-start | bytes 2359304 | tf_op jit(solution)/shard_map/ppermute | solution.py:346
  24.3 1.3 collective-permute-start.10
  25.6 1.3 collective-permute-start.6
  26.9 22.0 %collective-permute-done.10 = bf16[1024,128]{1,0:T(8,128)(2,1)} collective-permute-done((bf16[1024,128]{1,0:T(8,128)(2,1)S(1)}, bf16[1024,128]{1,0:T(8,128)(2,1)}, u32[]{:S(2)}, u32[]{:S(2)}) %collective-permute-start.10) | collective-permute-done | bytes 262176 | tf_op jit(solution)/shard_map/ppermute | solution.py:346
  48.9 1.3 collective-permute-start.11
  50.2 2.0 %collective-permute-start.7 = (bf16[1024,128]{1,0:T(8,128)(2,1)}, bf16[1024,128]{1,0:T(8,128)(2,1)S(1)}, u32[]{:S(2)}, u32[]{:S(2)}) collective-permute-start(bf16[1024,128]{1,0:T(8,128)(2,1)} %collective-permute-done.6), channel_id=1, source_target_pairs={{128,256},{320,192},{384,512},{576,448},{129,257},{321,193},{385,5... | collective-permute-start | bytes 786440 | tf_op jit(solution)/shard_map/ppermute | solution.py:346
  53.8 0.9 broadcast_select_fusion.2
  55.4 6.6 %collective-permute-start.4 = (bf16[1024,128]{1,0:T(8,128)(2,1)}, bf16[1024,128]{1,0:T(8,128)(2,1)S(1)}, u32[]{:S(2)}, u32[]{:S(2)}) collective-permute-start(bf16[1024,128]{1,0:T(8,128)(2,1)} %get-tuple-element.25), channel_id=1, source_target_pairs={{64,0},{128,64},{192,128},{320,256},{384,320},{448,384},{576,512},... | collective-permute-start | bytes 786440 | tf_op jit(solution)/shard_map/ppermute | solution.py:346
  62.0 12.2 %collective-permute-done.7.kz = bf16[1024,128]{1,0:T(8,128)(2,1)S(1)} collective-permute-done((bf16[1024,128]{1,0:T(8,128)(2,1)}, bf16[1024,128]{1,0:T(8,128)(2,1)S(1)}, u32[]{:S(2)}, u32[]{:S(2)}) %collective-permute-start.7) | collective-permute-done | bytes 262176 | tf_op jit(solution)/shard_map/ppermute | solution.py:346
  74.2 1.9 %collective-permute-start.3 = (bf16[1024,128]{1,0:T(8,128)(2,1)}, bf16[1024,128]{1,0:T(8,128)(2,1)}, u32[]{:S(2)}, u32[]{:S(2)}) collective-permute-start(bf16[1024,128]{1,0:T(8,128)(2,1)} %get-tuple-element.26), channel_id=1, source_target_pairs={{0,64},{64,128},{128,192},{256,320},{320,384},{384,448},{512,576},... | collective-permute-start | bytes 786440 | tf_op jit(solution)/shard_map/ppermute | solution.py:346
  77.0 6.2 %rowstats.1 = (f32[32,128]{1,0:T(8,128)}, f32[16,128]{1,0:T(8,128)}, f32[16,128]{1,0:T(8,128)}) custom-call(s32[1]{0:T(128)} %bitcast.shard, s32[768]{0:T(1024)} %reshape.46.nbr, s32[192]{0:T(256)} %cnt.5, bf16[2048,128]{1,0:T(8,128)(2,1)} %bitcast.49, bf16[2048,128]{1,0:T(8,128)(2,1)} %bitcast.41, bf16[2048,128]{1,0:T(8,128)(2,1)} %bitcast.51, ...), custom_call_target="tpu_custom_call" | custom-call | tf_op jit(solution)/shard_map/rowstats/pallas_call | solution.py:379
  83.2 14.0 %collective-permute-start.8 = (f32[16,128]{1,0:T(8,128)}, f32[16,128]{1,0:T(8,128)S(1)}, u32[]{:S(2)}, u32[]{:S(2)}) collective-permute-start(f32[16,128]{1,0:T(8,128)} %get-tuple-element.15), channel_id=1, source_target_pairs={{0,64},{64,128},{128,192},{192,256},{256,320},{320,384},{384,448},... | collective-permute-start | bytes 24584 | tf_op jit(solution)/shard_map/ppermute | solution.py:346
  97.2 1.0 collective-permute-done.8.slo
  98.2 1.9 %collective-permute-start.9 = (f32[16,128]{1,0:T(8,128)}, f32[16,128]{1,0:T(8,128)S(1)}, u32[]{:S(2)}, u32[]{:S(2)}) collective-permute-start(f32[16,128]{1,0:T(8,128)} %get-tuple-element.16), channel_id=1, source_target_pairs={{64,0},{128,64},{192,128},{256,192},{320,256},{384,320},{448,384},... | collective-permute-start | bytes 24584 | tf_op jit(solution)/shard_map/ppermute | solution.py:346
  100.1 9.9 %owngrads.1 = (bf16[64,32,128]{2,1,0:T(8,128)(2,1)}, f32[2048,128]{1,0:T(8,128)}, f32[2048,128]{1,0:T(8,128)}) custom-call(s32[1]{0:T(128)} %bitcast.shard, s32[768]{0:T(1024)} %reshape.46.nbr, s32[192]{0:T(256)} %cnt.5, bf16[2048,128]{1,0:T(8,128)(2,1)} %bitcast.50, bf16[2048,128]{1,0:T(8,128)(2,1)} %bitcast.42, bf16[2048,128]{1,0:T(8,128)(2,1)} %bitcast.47, ...), custom_call_target="tpu_custom_call" | custom-call | tf_op jit(solution)/shard_map/owngrads/pallas_call | solution.py:392
  110.9 9.3 %neargrads.1 = bf16[64,3,32,128]{3,2,1,0:T(8,128)(2,1)} custom-call(s32[1]{0:T(128)} %bitcast.shard, s32[768]{0:T(1024)} %reshape.46.nbr, s32[192]{0:T(256)} %cnt.5, bf16[2048,128]{1,0:T(8,128)(2,1)} %bitcast.43, bf16[2048,128]{1,0:T(8,128)(2,1)} %bitcast.48, bf16[3072,128]{1,0:T(8,128)(2,1)} %copy-done.1, bf16[3072,128]{1,0:T(8,128)(2,1)} %copy-done.2, ...), custom_call_target="tpu_custom_call" | custom-call | tf_op jit(solution)/shard_map/neargrads/pallas_call | solution.py:406
  120.2 55.8 %all_to_all.10 = bf16[64,3,32,128]{3,2,1,0:T(8,128)(2,1)S(1)} all-to-all(bf16[64,3,32,128]{3,2,1,0:T(8,128)(2,1)} %neargrads.1), channel_id=1, replica_groups=mesh['seq'=12,'head'=64] {'head'}, dimensions={0} | all-to-all | bytes 3145728 | tf_op jit(solution)/shard_map/all_to_all | solution.py:422
  176.5 0.9 reshape.55
  (54 shorter events, 6.8 us)
Async XLA Ops:
  0.6 16.2 %copy-start.5 = (bf16[2048,1,128]{2,0,1:T(8,128)(2,1)S(1)}, bf16[2048,1,128]{2,0,1:T(8,128)(2,1)}, u32[]{:S(2)}) copy-start(bf16[2048,1,128]{2,0,1:T(8,128)(2,1)} %param.7) | copy-start | bytes 1572868
  2.1 14.8 %copy-start = (bf16[2048,1,128]{2,0,1:T(8,128)(2,1)S(1)}, bf16[2048,1,128]{2,0,1:T(8,128)(2,1)}, u32[]{:S(2)}) copy-start(bf16[2048,1,128]{2,0,1:T(8,128)(2,1)} %param.8) | copy-start | bytes 1572868
  3.2 13.7 %copy-start.4 = (bf16[2048,1,128]{2,0,1:T(8,128)(2,1)S(1)}, bf16[2048,1,128]{2,0,1:T(8,128)(2,1)}, u32[]{:S(2)}) copy-start(bf16[2048,1,128]{2,0,1:T(8,128)(2,1)} %param.9) | copy-start | bytes 1572868
  3.2 49.0 %all-to-all-start = ((bf16[64,32,128]{2,1,0:T(8,128)(2,1)}), bf16[64,32,128]{2,1,0:T(8,128)(2,1)S(1)}, u32[]{:S(2)}, u32[]{:S(2)}) async-start(bf16[64,32,128]{2,1,0:T(8,128)(2,1)} %bitcast.40), calls=%async_computation | async-start | bytes 1048576 | tf_op jit(solution)/shard_map/all_to_all | solution.py:361
  18.0 34.2 %collective-permute-start = (bf16[3072,128]{1,0:T(8,128)(2,1)}, bf16[3072,128]{1,0:T(8,128)(2,1)S(1)}, u32[]{:S(2)}, u32[]{:S(2)}) collective-permute-start(bf16[3072,128]{1,0:T(8,128)(2,1)} %pad_maximum_fusion), channel_id=1, source_target_pairs={{0,64},{64,128},{128,192},{192,0},{256,320},{320,384},{384,448},{4... | collective-permute-start | bytes 2359304 | tf_op jit(solution)/shard_map/ppermute | solution.py:346
  22.0 30.2 %collective-permute-start.1 = (bf16[3072,128]{1,0:T(8,128)(2,1)}, bf16[3072,128]{1,0:T(8,128)(2,1)S(1)}, u32[]{:S(2)}, u32[]{:S(2)}) collective-permute-start(bf16[3072,128]{1,0:T(8,128)(2,1)} %pad_maximum_fusion.1), channel_id=1, source_target_pairs={{0,192},{64,0},{128,64},{192,128},{256,448},{320,256},{384,320},{4... | collective-permute-start | bytes 2359304 | tf_op jit(solution)/shard_map/ppermute | solution.py:346
  24.3 51.9 %copy-start.13 = (s32[192,4]{0,1:T(4,128)S(1)}, s32[192,4]{0,1:T(4,128)}, u32[]{:S(2)}) copy-start(s32[192,4]{0,1:T(4,128)} %param.12) | copy-start | bytes 9220
  24.3 24.6 %collective-permute-start.10 = (bf16[1024,128]{1,0:T(8,128)(2,1)S(1)}, bf16[1024,128]{1,0:T(8,128)(2,1)}, u32[]{:S(2)}, u32[]{:S(2)}) collective-permute-start(bf16[1024,128]{1,0:T(8,128)(2,1)S(1)} %broadcast_select_fusion), channel_id=1, source_target_pairs={{0,128},{192,64},{256,384},{448,320},{512,640},{704,576},{1,129},{... | collective-permute-start | bytes 786440 | tf_op jit(solution)/shard_map/ppermute | solution.py:346
  25.6 24.6 %collective-permute-start.6 = (bf16[1024,128]{1,0:T(8,128)(2,1)S(1)}, bf16[1024,128]{1,0:T(8,128)(2,1)}, u32[]{:S(2)}, u32[]{:S(2)}) collective-permute-start(bf16[1024,128]{1,0:T(8,128)(2,1)S(1)} %broadcast_select_fusion.1), channel_id=1, source_target_pairs={{0,64},{192,128},{256,320},{448,384},{512,576},{704,640},{1,65},{1... | collective-permute-start | bytes 786440 | tf_op jit(solution)/shard_map/ppermute | solution.py:346
  48.9 34.3 %collective-permute-start.11 = (bf16[1024,128]{1,0:T(8,128)(2,1)}, bf16[1024,128]{1,0:T(8,128)(2,1)S(1)}, u32[]{:S(2)}, u32[]{:S(2)}) collective-permute-start(bf16[1024,128]{1,0:T(8,128)(2,1)} %collective-permute-done.10), channel_id=1, source_target_pairs={{64,256},{320,512},{384,192},{640,448},{65,257},{321,513},{385,193... | collective-permute-start | bytes 786440 | tf_op jit(solution)/shard_map/ppermute | solution.py:346
  50.2 24.1 %collective-permute-start.7 = (bf16[1024,128]{1,0:T(8,128)(2,1)}, bf16[1024,128]{1,0:T(8,128)(2,1)S(1)}, u32[]{:S(2)}, u32[]{:S(2)}) collective-permute-start(bf16[1024,128]{1,0:T(8,128)(2,1)} %collective-permute-done.6), channel_id=1, source_target_pairs={{128,256},{320,192},{384,512},{576,448},{129,257},{321,193},{385,5... | collective-permute-start | bytes 786440 | tf_op jit(solution)/shard_map/ppermute | solution.py:346
  52.2 24.8 %copy-start.1 = (bf16[3072,128]{1,0:T(8,128)(2,1)}, bf16[3072,128]{1,0:T(8,128)(2,1)S(1)}, u32[]{:S(2)}) copy-start(bf16[3072,128]{1,0:T(8,128)(2,1)S(1)} %collective-permute-done.kv_lo.kvq_lo) | copy-start | bytes 2359300
  52.2 24.8 %copy-start.2 = (bf16[3072,128]{1,0:T(8,128)(2,1)}, bf16[3072,128]{1,0:T(8,128)(2,1)S(1)}, u32[]{:S(2)}) copy-start(bf16[3072,128]{1,0:T(8,128)(2,1)S(1)} %collective-permute-done.1.kv_hi.kvq_hi) | copy-start | bytes 2359300
  52.3 24.7 %copy-start.3 = (bf16[64,32,128]{2,1,0:T(8,128)(2,1)}, bf16[64,32,128]{2,1,0:T(8,128)(2,1)S(1)}, u32[]{:S(2)}) copy-start(bf16[64,32,128]{2,1,0:T(8,128)(2,1)S(1)} %all-to-all-done) | copy-start | bytes 1572868
  53.1 56.9 %collective-permute-start.2 = (bf16[1024,128]{1,0:T(8,128)(2,1)}, bf16[1024,128]{1,0:T(8,128)(2,1)S(1)}, u32[]{:S(2)}, u32[]{:S(2)}) collective-permute-start(bf16[1024,128]{1,0:T(8,128)(2,1)} %slice_select_fusion), channel_id=1, source_target_pairs={{0,256},{256,512},{448,192},{704,448},{1,257},{257,513},{449,193},... | collective-permute-start | bytes 786440 | tf_op jit(solution)/shard_map/ppermute | solution.py:346
  54.7 55.4 %collective-permute-start.5 = (bf16[1024,128]{1,0:T(8,128)(2,1)}, bf16[1024,128]{1,0:T(8,128)(2,1)S(1)}, u32[]{:S(2)}, u32[]{:S(2)}) collective-permute-start(bf16[1024,128]{1,0:T(8,128)(2,1)} %get-tuple-element.24), channel_id=1, source_target_pairs={{192,256},{256,192},{448,512},{512,448},{193,257},{257,193},{449,5... | collective-permute-start | bytes 786440 | tf_op jit(solution)/shard_map/ppermute | solution.py:346
  55.4 54.7 %collective-permute-start.4 = (bf16[1024,128]{1,0:T(8,128)(2,1)}, bf16[1024,128]{1,0:T(8,128)(2,1)S(1)}, u32[]{:S(2)}, u32[]{:S(2)}) collective-permute-start(bf16[1024,128]{1,0:T(8,128)(2,1)} %get-tuple-element.25), channel_id=1, source_target_pairs={{64,0},{128,64},{192,128},{320,256},{384,320},{448,384},{576,512},... | collective-permute-start | bytes 786440 | tf_op jit(solution)/shard_map/ppermute | solution.py:346
  74.2 2.8 %copy-start.6 = (bf16[1024,128]{1,0:T(8,128)(2,1)}, bf16[1024,128]{1,0:T(8,128)(2,1)S(1)}, u32[]{:S(2)}) copy-start(bf16[1024,128]{1,0:T(8,128)(2,1)S(1)} %collective-permute-done.7.kz) | copy-start | bytes 786436
  74.2 35.9 %collective-permute-start.3 = (bf16[1024,128]{1,0:T(8,128)(2,1)}, bf16[1024,128]{1,0:T(8,128)(2,1)}, u32[]{:S(2)}, u32[]{:S(2)}) collective-permute-start(bf16[1024,128]{1,0:T(8,128)(2,1)} %get-tuple-element.26), channel_id=1, source_target_pairs={{0,64},{64,128},{128,192},{256,320},{320,384},{384,448},{512,576},... | collective-permute-start | bytes 786440 | tf_op jit(solution)/shard_map/ppermute | solution.py:346
  83.2 16.9 %copy-start.8 = (bf16[1024,128]{1,0:T(8,128)(2,1)}, bf16[1024,128]{1,0:T(8,128)(2,1)S(1)}, u32[]{:S(2)}) copy-start(bf16[1024,128]{1,0:T(8,128)(2,1)S(1)} %collective-permute-done.11.vz) | copy-start | bytes 786436
  83.2 15.0 %collective-permute-start.8 = (f32[16,128]{1,0:T(8,128)}, f32[16,128]{1,0:T(8,128)S(1)}, u32[]{:S(2)}, u32[]{:S(2)}) collective-permute-start(f32[16,128]{1,0:T(8,128)} %get-tuple-element.15), channel_id=1, source_target_pairs={{0,64},{64,128},{128,192},{192,256},{256,320},{320,384},{384,448},... | collective-permute-start | bytes 24584 | tf_op jit(solution)/shard_map/ppermute | solution.py:346
  98.2 11.8 %copy-start.11 = (f32[16,128]{1,0:T(8,128)}, f32[16,128]{1,0:T(8,128)S(1)}, u32[]{:S(2)}) copy-start(f32[16,128]{1,0:T(8,128)S(1)} %collective-permute-done.8.slo) | copy-start | bytes 24580
  98.2 11.8 %collective-permute-start.9 = (f32[16,128]{1,0:T(8,128)}, f32[16,128]{1,0:T(8,128)S(1)}, u32[]{:S(2)}, u32[]{:S(2)}) collective-permute-start(f32[16,128]{1,0:T(8,128)} %get-tuple-element.16), channel_id=1, source_target_pairs={{64,0},{128,64},{192,128},{256,192},{320,256},{384,320},{448,384},... | collective-permute-start | bytes 24584 | tf_op jit(solution)/shard_map/ppermute | solution.py:346
  110.1 0.8 copy-start.10
  (3 other events, 2.1 us)
where the time goes:
time: 180 us
  blocking collectives  55.8 us (31%)
  starting transfers between devices  50.5 us (28%)
  waiting for transfers between devices  35.2 us (20%)
  Pallas kernels  25.3 us (14%)
  local copies, waits for them, and re-layouts  8 us (4%)
  other arithmetic  3.75 us (2%)
    all_to_all x1, blocking collectives, device_work(): lax.all_to_all(joint, 'head', split_axis=0, concat_axis=0, tiled=True)  55.8 us
    ppermute x12, starting transfers between devices, move(): return lax.ppermute(rows, 'seq', route[name])  36.9 us
    ppermute x12, waiting for transfers between devices, move(): return lax.ppermute(rows, 'seq', route[name])  35.2 us
    all_to_all x1, starting transfers between devices, device_work(): lax.all_to_all(sent, 'head', split_axis=0, concat_axis=0, tiled=True)  13.6 us
    pallas_call x1, Pallas kernels, device_work(): pl.pallas_call(own_kernel(tiles_dev, nbr_count, ring_len, peers), out_sha...  9.88 us
    pallas_call x1, Pallas kernels, device_work(): pl.pallas_call(near_kernel(tiles_dev, tiles_all, nbr_count, ring_len, pee...  9.25 us
    pallas_call x1, Pallas kernels, device_work(): pl.pallas_call(stats_kernel(tiles_dev, nbr_count, ring_len), out_shape=(j...  6.2 us
  transfers between devices with their start and end apart: 13, of which 3 were waited for; matrix products, arithmetic and copies ran while one was open for 3% of the time, Pallas kernels for 9%

commit v1 on v0

--- a/solution.py
+++ b/solution.py
@@ -8,6 +8,7 @@
 from jax.sharding import PartitionSpec as P
 
 TILE = 128
+STEP_PAIRS = 2
 NT = (((1,), (1,)), ((), ()))
 NN = (((1,), (0,)), ((), ()))
 TN = (((0,), (0,)), ((), ()))
@@ -216,7 +217,7 @@
     share = own // peers
 
     def kernel(
-        shard, nbr, cnt, k_any, v_any, kvq_lo, kvq_hi, qz, glo, ghi, gz, slo, shi, dq_any, dk_any, dv_any,
+        shard, nbr, cnt, k_any, v_any, qlo, qhi, qz, glo, ghi, gz, slo, shi, dq_any, dk_any, dv_any,
         joint, k, v, q_near, g_near, dk_acc, dv_acc, stats_near, pairs, sems,
     ):
         s = shard[0]
@@ -226,7 +227,6 @@
         at_high = col == ring_len - 1
         first_half = pl.ds(0, half)
         second_half = pl.ds(half, half)
-        third_half = pl.ds(2 * half, half)
         moves = (
             (k, (k_any,)),
             (v, (v_any,)),
@@ -234,8 +234,8 @@
             (dv_acc.at[pl.ds(0, own)], (dv_any,)),
             (stats_near.at[0], (slo,)),
             (stats_near.at[1], (shi,)),
-            (q_near.at[first_half], (qz, at_low, kvq_lo.at[third_half])),
-            (q_near.at[second_half], (qz, at_high, kvq_hi.at[third_half])),
+            (q_near.at[first_half], (qz, at_low, qlo)),
+            (q_near.at[second_half], (qz, at_high, qhi)),
             (g_near.at[first_half], (gz, at_low, glo)),
             (g_near.at[second_half], (gz, at_high, ghi)),
             (joint.at[:, 0], (dq_any,)),
@@ -257,8 +257,9 @@
             return count
 
         count = lax.fori_loop(0, tiles_dev, scan, jnp.int32(0))
-        pairs[0, count] = 0
-        pairs[1, count] = tiles_dev
+        for extra in range(STEP_PAIRS - 1):
+            pairs[0, count + extra] = 0
+            pairs[1, count + extra] = tiles_dev
         wait_copies(moves, sems)
 
         def near_terms(index):
@@ -277,14 +278,12 @@
             return mine, dot(dscore, q_t, NN), dot(prob, g_t, NN)
 
         def near_step(j, carry):
-            first = near_terms(2 * j)
-            second = near_terms(2 * j + 1)
-            for mine, dk, dv in (first, second):
+            for mine, dk, dv in [near_terms(STEP_PAIRS * j + i) for i in range(STEP_PAIRS)]:
                 dk_acc[span(mine), :] += dk
                 dv_acc[span(mine), :] += dv
             return carry
 
-        lax.fori_loop(0, (count + 1) // 2, near_step, 0)
+        lax.fori_loop(0, (count + STEP_PAIRS - 1) // STEP_PAIRS, near_step, 0)
         for which, acc in ((1, dk_acc), (2, dv_acc)):
             joint[:, which] = (
                 acc[pl.ds(0, own), :].astype(jnp.bfloat16).reshape(peers, share, TILE)
@@ -353,18 +352,19 @@
     v = value_rows.reshape(shard_tokens, head_dim)
     o = attn_output.reshape(shard_tokens, head_dim)
     table = neighbours.reshape(-1)
-    k_side = move(edge(k), "inward")
-    v_side = move(edge(v), "inward_two")
-    kvq_low = move(jnp.concatenate([k[half:], v[half:], q[half:]]), "around")
-    kvq_high = move(jnp.concatenate([k[:half], v[:half], q[:half]]), "around_back")
+    kv_low = move(jnp.concatenate([k[half:], v[half:]]), "around")
+    kv_high = move(jnp.concatenate([k[:half], v[:half]]), "around_back")
     sent = out_grad.reshape(seq_rows, peers, head_dim).transpose(1, 0, 2)
     grads = lax.all_to_all(sent, "head", split_axis=0, concat_axis=0, tiled=True)
     grads = grads.reshape(shard_tokens, head_dim)
-    k_far = move(k_side, "outward")
+    k_far = move(jnp.where(at_start, kv_low[:half], kv_high[:half]), "far")
+    v_side = move(edge(v), "inward_two")
+    q_side = move(edge(q), "inward")
     v_far = move(v_side, "outward_two")
-    q_low, q_high, grads = lax.optimization_barrier((kvq_low, kvq_high, grads))
-    q_far = move(jnp.where(at_start, q_low[2 * half :], q_high[2 * half :]), "far")
+    q_far = move(q_side, "outward")
     g_far = move(edge(grads), "cross")
+    q_low = move(q[half:], "up")
+    q_high = move(q[:half], "down")
     g_low = move(grads[half:], "up")
     g_high = move(grads[:half], "down")
 
@@ -385,7 +385,7 @@
         out_specs=(vmem,) * 3,
         scratch_shapes=[held, held, held, wide, pltpu.SemaphoreType.DMA((6,))],
         name="rowstats",
-    )(place, table, counts, q, k, o, grads, kvq_low, kvq_high, k_far)
+    )(place, table, counts, q, k, o, grads, kv_low, kv_high, k_far)
     near_low = move(stat_high, "forward")
     near_high = move(stat_low, "backward")
     sums = jax.ShapeDtypeStruct((shard_tokens, head_dim), jnp.float32)
@@ -402,7 +402,7 @@
             pltpu.SemaphoreType.DMA((9,)),
         ],
         name="owngrads",
-    )(place, table, counts, q, k, v, grads, kvq_low, kvq_high, k_far, v_far, stat_all)
+    )(place, table, counts, q, k, v, grads, kv_low, kv_high, k_far, v_far, stat_all)
     joint = pl.pallas_call(
         near_kernel(tiles_dev, tiles_all, nbr_count, ring_len, peers),
         out_shape=jax.ShapeDtypeStruct((peers, 3, seq_rows, head_dim), jnp.bfloat16),
@@ -416,7 +416,7 @@
         ],
         name="neargrads",
     )(
-        place, table, counts, k, v, kvq_low, kvq_high, q_far, g_low, g_high, g_far,
+        place, table, counts, k, v, q_low, q_high, q_far, g_low, g_high, g_far,
         near_low, near_high, dq, dk, dv,
     )
     back = lax.all_to_all(joint, "head", split_axis=0, concat_axis=0, tiled=True)

time: 180 us -> 169 us (0.939)
  the two profiles are of different devices: /device:TPU:259 before, /device:TPU:257 now
where the time goes in v1:
time: 169 us; the launch traced here: 168 us
  starting transfers between devices  71.6 us (42%)
  blocking collectives  53.5 us (32%)
  Pallas kernels  23.9 us (14%)
  waiting for transfers between devices  8.68 us (5%)
  local copies, waits for them, and re-layouts  8.62 us (5%)
    ppermute x14, starting transfers between devices, move(): return lax.ppermute(rows, 'seq', route[name])  58.1 us
    all_to_all x1, blocking collectives, device_work(): lax.all_to_all(joint, 'head', split_axis=0, concat_axis=0, tiled=True)  53.5 us
    all_to_all x1, starting transfers between devices, device_work(): lax.all_to_all(sent, 'head', split_axis=0, concat_axis=0, tiled=True)  13.5 us
    pallas_call x1, Pallas kernels, device_work(): pl.pallas_call(own_kernel(tiles_dev, nbr_count, ring_len, peers), out_sha...  9.86 us
    ppermute x14, waiting for transfers between devices, move(): return lax.ppermute(rows, 'seq', route[name])  8.68 us
    pallas_call x1, Pallas kernels, device_work(): pl.pallas_call(near_kernel(tiles_dev, tiles_all, nbr_count, ring_len, pee...  7.81 us
    pallas_call x1, Pallas kernels, device_work(): pl.pallas_call(stats_kernel(tiles_dev, nbr_count, ring_len), out_shape=(j...  6.19 us
  transfers between devices with their start and end apart: 15, of which 3 were waited for; matrix products, arithmetic and copies ran while one was open for 2% of the time, Pallas kernels for 10%

profile of v1, /device:TPU:257, one launch (start us, length us, event | category | flops | bytes accessed | tf_op | source)
XLA Modules:
  0.0 168.3 jit_solution(18048708421067297057)
XLA Ops:
  0.6 1.4 reshape.51
  2.1 1.1 copy.17
  3.2 13.5 %all-to-all-start = ((bf16[64,32,128]{2,1,0:T(8,128)(2,1)}), bf16[64,32,128]{2,1,0:T(8,128)(2,1)S(1)}, u32[]{:S(2)}, u32[]{:S(2)}) async-start(bf16[64,32,128]{2,1,0:T(8,128)(2,1)} %bitcast.44), calls=%async_computation | async-start | bytes 1048576 | tf_op jit(solution)/shard_map/all_to_all | solution.py:358
  16.9 3.3 %collective-permute-start.7 = (bf16[2048,128]{1,0:T(8,128)(2,1)S(1)}, bf16[2048,128]{1,0:T(8,128)(2,1)S(1)}, u32[]{:S(2)}, u32[]{:S(2)}) collective-permute-start(bf16[2048,128]{1,0:T(8,128)(2,1)S(1)} %pad_maximum_fusion), channel_id=1, source_target_pairs={{0,64},{64,128},{128,192},{192,0},{256,320},{320,384},{384,448},{4... | collective-permute-start | bytes 1572872 | tf_op jit(solution)/shard_map/ppermute | solution.py:345
  20.9 3.4 %collective-permute-start.8 = (bf16[2048,128]{1,0:T(8,128)(2,1)}, bf16[2048,128]{1,0:T(8,128)(2,1)S(1)}, u32[]{:S(2)}, u32[]{:S(2)}) collective-permute-start(bf16[2048,128]{1,0:T(8,128)(2,1)} %pad_maximum_fusion.1), channel_id=1, source_target_pairs={{0,192},{64,0},{128,64},{192,128},{256,448},{320,256},{384,320},{4... | collective-permute-start | bytes 1572872 | tf_op jit(solution)/shard_map/ppermute | solution.py:345
  24.4 4.2 %collective-permute-start.12 = (bf16[1024,128]{1,0:T(8,128)(2,1)S(1)}, bf16[1024,128]{1,0:T(8,128)(2,1)}, u32[]{:S(2)}, u32[]{:S(2)}) collective-permute-start(bf16[1024,128]{1,0:T(8,128)(2,1)S(1)} %broadcast_select_fusion), channel_id=1, source_target_pairs={{0,128},{192,64},{256,384},{448,320},{512,640},{704,576},{1,129},{... | collective-permute-start | bytes 786440 | tf_op jit(solution)/shard_map/ppermute | solution.py:345
  28.6 2.0 %collective-permute-start.2 = (bf16[1024,128]{1,0:T(8,128)(2,1)S(1)}, bf16[1024,128]{1,0:T(8,128)(2,1)}, u32[]{:S(2)}, u32[]{:S(2)}) collective-permute-start(bf16[1024,128]{1,0:T(8,128)(2,1)S(1)} %broadcast_select_fusion.2), channel_id=1, source_target_pairs={{0,64},{192,128},{256,320},{448,384},{512,576},{704,640},{1,65},{1... | collective-permute-start | bytes 786440 | tf_op jit(solution)/shard_map/ppermute | solution.py:345
  31.3 2.1 %collective-permute-start = (bf16[1024,128]{1,0:T(8,128)(2,1)}, bf16[1024,128]{1,0:T(8,128)(2,1)}, u32[]{:S(2)}, u32[]{:S(2)}) collective-permute-start(bf16[1024,128]{1,0:T(8,128)(2,1)} %get-tuple-element.25), channel_id=1, source_target_pairs={{0,64},{64,128},{128,192},{256,320},{320,384},{384,448},{512,576},... | collective-permute-start | bytes 786440 | tf_op jit(solution)/shard_map/ppermute | solution.py:345
  33.4 3.2 %collective-permute-done.12 = bf16[1024,128]{1,0:T(8,128)(2,1)} collective-permute-done((bf16[1024,128]{1,0:T(8,128)(2,1)S(1)}, bf16[1024,128]{1,0:T(8,128)(2,1)}, u32[]{:S(2)}, u32[]{:S(2)}) %collective-permute-start.12) | collective-permute-done | bytes 262176 | tf_op jit(solution)/shard_map/ppermute | solution.py:345
  36.6 1.3 collective-permute-start.1
  37.9 4.3 %collective-permute-done.2 = bf16[1024,128]{1,0:T(8,128)(2,1)} collective-permute-done((bf16[1024,128]{1,0:T(8,128)(2,1)S(1)}, bf16[1024,128]{1,0:T(8,128)(2,1)}, u32[]{:S(2)}, u32[]{:S(2)}) %collective-permute-start.2) | collective-permute-done | bytes 262176 | tf_op jit(solution)/shard_map/ppermute | solution.py:345
  42.2 1.3 collective-permute-start.13
  43.5 1.3 collective-permute-start.3
  44.9 5.8 %collective-permute-start.9 = (bf16[1024,128]{1,0:T(8,128)(2,1)S(1)}, bf16[1024,128]{1,0:T(8,128)(2,1)S(1)}, u32[]{:S(2)}, u32[]{:S(2)}) collective-permute-start(bf16[1024,128]{1,0:T(8,128)(2,1)S(1)} %slice_select_fusion), channel_id=1, source_target_pairs={{0,256},{256,512},{448,192},{704,448},{1,257},{257,513},{449,193},... | collective-permute-start | bytes 786440 | tf_op jit(solution)/shard_map/ppermute | solution.py:345
  50.9 1.9 %collective-permute-start.6 = (bf16[1024,128]{1,0:T(8,128)(2,1)S(1)}, bf16[1024,128]{1,0:T(8,128)(2,1)}, u32[]{:S(2)}, u32[]{:S(2)}) collective-permute-start(bf16[1024,128]{1,0:T(8,128)(2,1)S(1)} %broadcast_select_fusion.1), channel_id=1, source_target_pairs={{192,256},{256,192},{448,512},{512,448},{193,257},{257,193},{449,5... | collective-permute-start | bytes 786440 | tf_op jit(solution)/shard_map/ppermute | solution.py:345
  52.8 2.6 %collective-permute-start.4 = (bf16[1024,128]{1,0:T(8,128)(2,1)S(1)}, bf16[1024,128]{1,0:T(8,128)(2,1)S(1)}, u32[]{:S(2)}, u32[]{:S(2)}) collective-permute-start(bf16[1024,128]{1,0:T(8,128)(2,1)S(1)} %bitcast.55), channel_id=1, source_target_pairs={{0,64},{64,128},{128,192},{256,320},{320,384},{384,448},{512,576},... | collective-permute-start | bytes 786440 | tf_op jit(solution)/shard_map/ppermute | solution.py:345
  55.4 1.1 collective-permute-done.9.kz
  56.5 1.3 collective-permute-start.5
  58.7 6.2 %rowstats.1 = (f32[32,128]{1,0:T(8,128)}, f32[16,128]{1,0:T(8,128)}, f32[16,128]{1,0:T(8,128)}) custom-call(s32[1]{0:T(128)} %bitcast.shard, s32[768]{0:T(1024)} %reshape.48.nbr, s32[192]{0:T(256)} %cnt.5, bf16[2048,128]{1,0:T(8,128)(2,1)} %bitcast.45, bf16[2048,128]{1,0:T(8,128)(2,1)} %bitcast.51, bf16[2048,128]{1,0:T(8,128)(2,1)} %bitcast.56, ...), custom_call_target="tpu_custom_call" | custom-call | tf_op jit(solution)/shard_map/rowstats/pallas_call | solution.py:379
  64.9 4.0 %collective-permute-start.10 = (f32[16,128]{1,0:T(8,128)}, f32[16,128]{1,0:T(8,128)S(1)}, u32[]{:S(2)}, u32[]{:S(2)}) collective-permute-start(f32[16,128]{1,0:T(8,128)} %get-tuple-element.9), channel_id=1, source_target_pairs={{0,64},{64,128},{128,192},{192,256},{256,320},{320,384},{384,448},... | collective-permute-start | bytes 24584 | tf_op jit(solution)/shard_map/ppermute | solution.py:345
  68.9 23.8 %collective-permute-start.11 = (f32[16,128]{1,0:T(8,128)}, f32[16,128]{1,0:T(8,128)S(1)}, u32[]{:S(2)}, u32[]{:S(2)}) collective-permute-start(f32[16,128]{1,0:T(8,128)} %get-tuple-element.10), channel_id=1, source_target_pairs={{64,0},{128,64},{192,128},{256,192},{320,256},{384,320},{448,384},... | collective-permute-start | bytes 24584 | tf_op jit(solution)/shard_map/ppermute | solution.py:345
  92.7 9.9 %owngrads.1 = (bf16[64,32,128]{2,1,0:T(8,128)(2,1)}, f32[2048,128]{1,0:T(8,128)}, f32[2048,128]{1,0:T(8,128)}) custom-call(s32[1]{0:T(128)} %bitcast.shard, s32[768]{0:T(1024)} %reshape.48.nbr, s32[192]{0:T(256)} %cnt.5, bf16[2048,128]{1,0:T(8,128)(2,1)} %bitcast.46, bf16[2048,128]{1,0:T(8,128)(2,1)} %bitcast.52, bf16[2048,128]{1,0:T(8,128)(2,1)} %bitcast.49, ...), custom_call_target="tpu_custom_call" | custom-call | tf_op jit(solution)/shard_map/owngrads/pallas_call | solution.py:392
  103.4 7.8 %neargrads.1 = bf16[64,3,32,128]{3,2,1,0:T(8,128)(2,1)} custom-call(s32[1]{0:T(128)} %bitcast.shard, s32[768]{0:T(1024)} %reshape.48.nbr, s32[192]{0:T(256)} %cnt.5, bf16[2048,128]{1,0:T(8,128)(2,1)} %bitcast.53, bf16[2048,128]{1,0:T(8,128)(2,1)} %bitcast.50, bf16[1024,128]{1,0:T(8,128)(2,1)} %collective-permute-done.qlo, ...), custom_call_target="tpu_custom_call" | custom-call | tf_op jit(solution)/shard_map/neargrads/pallas_call | solution.py:406
  111.2 53.5 %all_to_all.10 = bf16[64,3,32,128]{3,2,1,0:T(8,128)(2,1)S(1)} all-to-all(bf16[64,3,32,128]{3,2,1,0:T(8,128)(2,1)} %neargrads.1), channel_id=1, replica_groups=mesh['seq'=12,'head'=64] {'head'}, dimensions={0} | all-to-all | bytes 3145728 | tf_op jit(solution)/shard_map/all_to_all | solution.py:422
  (55 shorter events, 7.1 us)
Async XLA Ops:
  0.6 16.1 %copy-start.3 = (bf16[2048,1,128]{2,0,1:T(8,128)(2,1)S(1)}, bf16[2048,1,128]{2,0,1:T(8,128)(2,1)}, u32[]{:S(2)}) copy-start(bf16[2048,1,128]{2,0,1:T(8,128)(2,1)} %param.8) | copy-start | bytes 1572868
  2.1 14.7 %copy-start.2 = (bf16[2048,1,128]{2,0,1:T(8,128)(2,1)S(1)}, bf16[2048,1,128]{2,0,1:T(8,128)(2,1)}, u32[]{:S(2)}) copy-start(bf16[2048,1,128]{2,0,1:T(8,128)(2,1)} %param.9) | copy-start | bytes 1572868
  3.2 47.5 %all-to-all-start = ((bf16[64,32,128]{2,1,0:T(8,128)(2,1)}), bf16[64,32,128]{2,1,0:T(8,128)(2,1)S(1)}, u32[]{:S(2)}, u32[]{:S(2)}) async-start(bf16[64,32,128]{2,1,0:T(8,128)(2,1)} %bitcast.44), calls=%async_computation | async-start | bytes 1048576 | tf_op jit(solution)/shard_map/all_to_all | solution.py:358
  16.8 11.7 %copy-start = (bf16[2048,1,128]{2,0,1:T(8,128)(2,1)S(1)}, bf16[2048,1,128]{2,0,1:T(8,128)(2,1)}, u32[]{:S(2)}) copy-start(bf16[2048,1,128]{2,0,1:T(8,128)(2,1)} %param.7) | copy-start | bytes 1572868
  16.9 26.6 %collective-permute-start.7 = (bf16[2048,128]{1,0:T(8,128)(2,1)S(1)}, bf16[2048,128]{1,0:T(8,128)(2,1)S(1)}, u32[]{:S(2)}, u32[]{:S(2)}) collective-permute-start(bf16[2048,128]{1,0:T(8,128)(2,1)S(1)} %pad_maximum_fusion), channel_id=1, source_target_pairs={{0,64},{64,128},{128,192},{192,0},{256,320},{320,384},{384,448},{4... | collective-permute-start | bytes 1572872 | tf_op jit(solution)/shard_map/ppermute | solution.py:345
  20.9 23.9 %collective-permute-start.8 = (bf16[2048,128]{1,0:T(8,128)(2,1)}, bf16[2048,128]{1,0:T(8,128)(2,1)S(1)}, u32[]{:S(2)}, u32[]{:S(2)}) collective-permute-start(bf16[2048,128]{1,0:T(8,128)(2,1)} %pad_maximum_fusion.1), channel_id=1, source_target_pairs={{0,192},{64,0},{128,64},{192,128},{256,448},{320,256},{384,320},{4... | collective-permute-start | bytes 1572872 | tf_op jit(solution)/shard_map/ppermute | solution.py:345
  24.4 12.2 %collective-permute-start.12 = (bf16[1024,128]{1,0:T(8,128)(2,1)S(1)}, bf16[1024,128]{1,0:T(8,128)(2,1)}, u32[]{:S(2)}, u32[]{:S(2)}) collective-permute-start(bf16[1024,128]{1,0:T(8,128)(2,1)S(1)} %broadcast_select_fusion), channel_id=1, source_target_pairs={{0,128},{192,64},{256,384},{448,320},{512,640},{704,576},{1,129},{... | collective-permute-start | bytes 786440 | tf_op jit(solution)/shard_map/ppermute | solution.py:345
  28.6 13.6 %collective-permute-start.2 = (bf16[1024,128]{1,0:T(8,128)(2,1)S(1)}, bf16[1024,128]{1,0:T(8,128)(2,1)}, u32[]{:S(2)}, u32[]{:S(2)}) collective-permute-start(bf16[1024,128]{1,0:T(8,128)(2,1)S(1)} %broadcast_select_fusion.2), channel_id=1, source_target_pairs={{0,64},{192,128},{256,320},{448,384},{512,576},{704,640},{1,65},{1... | collective-permute-start | bytes 786440 | tf_op jit(solution)/shard_map/ppermute | solution.py:345
  31.3 26.5 %copy-start.11 = (s32[192,4]{0,1:T(4,128)S(1)}, s32[192,4]{0,1:T(4,128)}, u32[]{:S(2)}) copy-start(s32[192,4]{0,1:T(4,128)} %param.12) | copy-start | bytes 9220
  31.3 19.6 %collective-permute-start = (bf16[1024,128]{1,0:T(8,128)(2,1)}, bf16[1024,128]{1,0:T(8,128)(2,1)}, u32[]{:S(2)}, u32[]{:S(2)}) collective-permute-start(bf16[1024,128]{1,0:T(8,128)(2,1)} %get-tuple-element.25), channel_id=1, source_target_pairs={{0,64},{64,128},{128,192},{256,320},{320,384},{384,448},{512,576},... | collective-permute-start | bytes 786440 | tf_op jit(solution)/shard_map/ppermute | solution.py:345
  36.6 16.2 %collective-permute-start.1 = (bf16[1024,128]{1,0:T(8,128)(2,1)S(1)}, bf16[1024,128]{1,0:T(8,128)(2,1)}, u32[]{:S(2)}, u32[]{:S(2)}) collective-permute-start(bf16[1024,128]{1,0:T(8,128)(2,1)S(1)} %get-tuple-element.24), channel_id=1, source_target_pairs={{64,0},{128,64},{192,128},{320,256},{384,320},{448,384},{576,512},... | collective-permute-start | bytes 786440 | tf_op jit(solution)/shard_map/ppermute | solution.py:345
  42.2 22.7 %collective-permute-start.13 = (bf16[1024,128]{1,0:T(8,128)(2,1)}, bf16[1024,128]{1,0:T(8,128)(2,1)}, u32[]{:S(2)}, u32[]{:S(2)}) collective-permute-start(bf16[1024,128]{1,0:T(8,128)(2,1)} %collective-permute-done.12), channel_id=1, source_target_pairs={{64,256},{320,512},{384,192},{640,448},{65,257},{321,513},{385,193... | collective-permute-start | bytes 786440 | tf_op jit(solution)/shard_map/ppermute | solution.py:345
  43.5 15.2 %copy-start.4 = (bf16[2048,128]{1,0:T(8,128)(2,1)}, bf16[2048,128]{1,0:T(8,128)(2,1)S(1)}, u32[]{:S(2)}) copy-start(bf16[2048,128]{1,0:T(8,128)(2,1)S(1)} %collective-permute-done.7.kv_lo) | copy-start | bytes 1572868
  43.5 25.4 %collective-permute-start.3 = (bf16[1024,128]{1,0:T(8,128)(2,1)}, bf16[1024,128]{1,0:T(8,128)(2,1)S(1)}, u32[]{:S(2)}, u32[]{:S(2)}) collective-permute-start(bf16[1024,128]{1,0:T(8,128)(2,1)} %collective-permute-done.2), channel_id=1, source_target_pairs={{128,256},{320,192},{384,512},{576,448},{129,257},{321,193},{385,5... | collective-permute-start | bytes 786440 | tf_op jit(solution)/shard_map/ppermute | solution.py:345
  44.8 13.9 %copy-start.5 = (bf16[2048,128]{1,0:T(8,128)(2,1)}, bf16[2048,128]{1,0:T(8,128)(2,1)S(1)}, u32[]{:S(2)}) copy-start(bf16[2048,128]{1,0:T(8,128)(2,1)S(1)} %collective-permute-done.8.kv_hi) | copy-start | bytes 1572868
  44.9 11.7 %collective-permute-start.9 = (bf16[1024,128]{1,0:T(8,128)(2,1)S(1)}, bf16[1024,128]{1,0:T(8,128)(2,1)S(1)}, u32[]{:S(2)}, u32[]{:S(2)}) collective-permute-start(bf16[1024,128]{1,0:T(8,128)(2,1)S(1)} %slice_select_fusion), channel_id=1, source_target_pairs={{0,256},{256,512},{448,192},{704,448},{1,257},{257,513},{449,193},... | collective-permute-start | bytes 786440 | tf_op jit(solution)/shard_map/ppermute | solution.py:345
  50.7 8.0 %copy-start.1 = (bf16[64,32,128]{2,1,0:T(8,128)(2,1)}, bf16[64,32,128]{2,1,0:T(8,128)(2,1)S(1)}, u32[]{:S(2)}) copy-start(bf16[64,32,128]{2,1,0:T(8,128)(2,1)S(1)} %all-to-all-done) | copy-start | bytes 1572868
  50.9 51.8 %collective-permute-start.6 = (bf16[1024,128]{1,0:T(8,128)(2,1)S(1)}, bf16[1024,128]{1,0:T(8,128)(2,1)}, u32[]{:S(2)}, u32[]{:S(2)}) collective-permute-start(bf16[1024,128]{1,0:T(8,128)(2,1)S(1)} %broadcast_select_fusion.1), channel_id=1, source_target_pairs={{192,256},{256,192},{448,512},{512,448},{193,257},{257,193},{449,5... | collective-permute-start | bytes 786440 | tf_op jit(solution)/shard_map/ppermute | solution.py:345
  52.8 49.9 %collective-permute-start.4 = (bf16[1024,128]{1,0:T(8,128)(2,1)S(1)}, bf16[1024,128]{1,0:T(8,128)(2,1)S(1)}, u32[]{:S(2)}, u32[]{:S(2)}) collective-permute-start(bf16[1024,128]{1,0:T(8,128)(2,1)S(1)} %bitcast.55), channel_id=1, source_target_pairs={{0,64},{64,128},{128,192},{256,320},{320,384},{384,448},{512,576},... | collective-permute-start | bytes 786440 | tf_op jit(solution)/shard_map/ppermute | solution.py:345
  56.5 2.1 %copy-start.6 = (bf16[1024,128]{1,0:T(8,128)(2,1)}, bf16[1024,128]{1,0:T(8,128)(2,1)S(1)}, u32[]{:S(2)}) copy-start(bf16[1024,128]{1,0:T(8,128)(2,1)S(1)} %collective-permute-done.9.kz) | copy-start | bytes 786436
  56.5 46.1 %collective-permute-start.5 = (bf16[1024,128]{1,0:T(8,128)(2,1)S(1)}, bf16[1024,128]{1,0:T(8,128)(2,1)}, u32[]{:S(2)}, u32[]{:S(2)}) collective-permute-start(bf16[1024,128]{1,0:T(8,128)(2,1)S(1)} %bitcast.54), channel_id=1, source_target_pairs={{64,0},{128,64},{192,128},{320,256},{384,320},{448,384},{576,512},... | collective-permute-start | bytes 786440 | tf_op jit(solution)/shard_map/ppermute | solution.py:345
  64.9 37.7 %collective-permute-start.10 = (f32[16,128]{1,0:T(8,128)}, f32[16,128]{1,0:T(8,128)S(1)}, u32[]{:S(2)}, u32[]{:S(2)}) collective-permute-start(f32[16,128]{1,0:T(8,128)} %get-tuple-element.9), channel_id=1, source_target_pairs={{0,64},{64,128},{128,192},{192,256},{256,320},{320,384},{384,448},... | collective-permute-start | bytes 24584 | tf_op jit(solution)/shard_map/ppermute | solution.py:345
  68.9 33.7 %copy-start.7 = (bf16[1024,128]{1,0:T(8,128)(2,1)}, bf16[1024,128]{1,0:T(8,128)(2,1)S(1)}, u32[]{:S(2)}) copy-start(bf16[1024,128]{1,0:T(8,128)(2,1)S(1)} %collective-permute-done.3.qz) | copy-start | bytes 786436
  68.9 33.7 %collective-permute-start.11 = (f32[16,128]{1,0:T(8,128)}, f32[16,128]{1,0:T(8,128)S(1)}, u32[]{:S(2)}, u32[]{:S(2)}) collective-permute-start(f32[16,128]{1,0:T(8,128)} %get-tuple-element.10), channel_id=1, source_target_pairs={{64,0},{128,64},{192,128},{256,192},{320,256},{384,320},{448,384},... | collective-permute-start | bytes 24584 | tf_op jit(solution)/shard_map/ppermute | solution.py:345
  (3 other events, 1.9 us)

commit v2 on v1

--- a/solution.py
+++ b/solution.py
@@ -8,7 +8,6 @@
 from jax.sharding import PartitionSpec as P
 
 TILE = 128
-STEP_PAIRS = 2
 NT = (((1,), (1,)), ((), ()))
 NN = (((1,), (0,)), ((), ()))
 TN = (((0,), (0,)), ((), ()))
@@ -217,7 +216,7 @@
     share = own // peers
 
     def kernel(
-        shard, nbr, cnt, k_any, v_any, qlo, qhi, qz, glo, ghi, gz, slo, shi, dq_any, dk_any, dv_any,
+        shard, nbr, cnt, k_any, v_any, qg_lo, qg_hi, qz, gz, slo, shi, dq_any, dk_any, dv_any,
         joint, k, v, q_near, g_near, dk_acc, dv_acc, stats_near, pairs, sems,
     ):
         s = shard[0]
@@ -234,10 +233,10 @@
             (dv_acc.at[pl.ds(0, own)], (dv_any,)),
             (stats_near.at[0], (slo,)),
             (stats_near.at[1], (shi,)),
-            (q_near.at[first_half], (qz, at_low, qlo)),
-            (q_near.at[second_half], (qz, at_high, qhi)),
-            (g_near.at[first_half], (gz, at_low, glo)),
-            (g_near.at[second_half], (gz, at_high, ghi)),
+            (q_near.at[first_half], (qz, at_low, qg_lo.at[first_half])),
+            (q_near.at[second_half], (qz, at_high, qg_hi.at[first_half])),
+            (g_near.at[first_half], (gz, at_low, qg_lo.at[second_half])),
+            (g_near.at[second_half], (gz, at_high, qg_hi.at[second_half])),
             (joint.at[:, 0], (dq_any,)),
         )
         start_copies(moves, sems)
@@ -257,10 +256,9 @@
             return count
 
         count = lax.fori_loop(0, tiles_dev, scan, jnp.int32(0))
-        for extra in range(STEP_PAIRS - 1):
-            pairs[0, count + extra] = 0
-            pairs[1, count + extra] = tiles_dev
-        wait_copies(moves, sems)
+        pairs[0, count] = 0
+        pairs[1, count] = tiles_dev
+        wait_copies(moves[:-1], sems)
 
         def near_terms(index):
             i = pairs[0, index]
@@ -278,12 +276,15 @@
             return mine, dot(dscore, q_t, NN), dot(prob, g_t, NN)
 
         def near_step(j, carry):
-            for mine, dk, dv in [near_terms(STEP_PAIRS * j + i) for i in range(STEP_PAIRS)]:
+            first = near_terms(2 * j)
+            second = near_terms(2 * j + 1)
+            for mine, dk, dv in (first, second):
                 dk_acc[span(mine), :] += dk
                 dv_acc[span(mine), :] += dv
             return carry
 
-        lax.fori_loop(0, (count + STEP_PAIRS - 1) // STEP_PAIRS, near_step, 0)
+        lax.fori_loop(0, (count + 1) // 2, near_step, 0)
+        pltpu.make_async_copy(dq_any, joint.at[:, 0], sems.at[len(moves) - 1]).wait()
         for which, acc in ((1, dk_acc), (2, dv_acc)):
             joint[:, which] = (
                 acc[pl.ds(0, own), :].astype(jnp.bfloat16).reshape(peers, share, TILE)
@@ -363,10 +364,8 @@
     v_far = move(v_side, "outward_two")
     q_far = move(q_side, "outward")
     g_far = move(edge(grads), "cross")
-    q_low = move(q[half:], "up")
-    q_high = move(q[:half], "down")
-    g_low = move(grads[half:], "up")
-    g_high = move(grads[:half], "down")
+    qg_low = move(jnp.concatenate([q[half:], grads[half:]]), "up")
+    qg_high = move(jnp.concatenate([q[:half], grads[:half]]), "down")
 
     smem = pl.BlockSpec(memory_space=pltpu.SMEM)
     vmem = pl.BlockSpec(memory_space=pltpu.VMEM)
@@ -406,7 +405,7 @@
     joint = pl.pallas_call(
         near_kernel(tiles_dev, tiles_all, nbr_count, ring_len, peers),
         out_shape=jax.ShapeDtypeStruct((peers, 3, seq_rows, head_dim), jnp.bfloat16),
-        in_specs=[smem] * 3 + [hbm] * 13,
+        in_specs=[smem] * 3 + [hbm] * 11,
         out_specs=vmem,
         scratch_shapes=[
             held, held, held, held, acc, acc,
@@ -416,7 +415,7 @@
         ],
         name="neargrads",
     )(
-        place, table, counts, k, v, q_low, q_high, q_far, g_low, g_high, g_far,
+        place, table, counts, k, v, qg_low, qg_high, q_far, g_far,
         near_low, near_high, dq, dk, dv,
     )
     back = lax.all_to_all(joint, "head", split_axis=0, concat_axis=0, tiled=True)

time: 169 us -> 165 us (0.976)
  waiting for transfers between devices: 8.68 us -> 3.82 us
  other arithmetic: 1.02 us -> 4.07 us
    ppermute x14 -> x12, waiting for transfers between devices: 8.68 us -> 3.82 us  [move(): return lax.ppermute(rows, 'seq', route[name])]
    ppermute x14 -> x12, starting transfers between devices: 58.1 us -> 56.8 us  [move(): return lax.ppermute(rows, 'seq', route[name])]
  transfers between devices with their start and end apart: 15 -> 13, of which waited for: 3 -> 2; matrix products, arithmetic and copies ran while one was open for 2% -> 3% of each run, Pallas kernels for 10% -> 10%
where the time goes in v2:
time: 165 us; the launch traced here: 164 us
  starting transfers between devices  70.3 us (43%)
  blocking collectives  53.5 us (32%)
  Pallas kernels  23.7 us (14%)
  local copies, waits for them, and re-layouts  7.9 us (5%)
  other arithmetic  4.07 us (2%)
  waiting for transfers between devices  3.82 us (2%)
    ppermute x12, starting transfers between devices, move(): return lax.ppermute(rows, 'seq', route[name])  56.8 us
    all_to_all x1, blocking collectives, device_work(): lax.all_to_all(joint, 'head', split_axis=0, concat_axis=0, tiled=True)  53.5 us
    all_to_all x1, starting transfers between devices, device_work(): lax.all_to_all(sent, 'head', split_axis=0, concat_axis=0, tiled=True)  13.5 us
    pallas_call x1, Pallas kernels, device_work(): pl.pallas_call(own_kernel(tiles_dev, nbr_count, ring_len, peers), out_sha...  9.86 us
    pallas_call x1, Pallas kernels, device_work(): pl.pallas_call(near_kernel(tiles_dev, tiles_all, nbr_count, ring_len, pee...  7.65 us
    pallas_call x1, Pallas kernels, device_work(): pl.pallas_call(stats_kernel(tiles_dev, nbr_count, ring_len), out_shape=(j...  6.19 us
    ppermute x12, waiting for transfers between devices, move(): return lax.ppermute(rows, 'seq', route[name])  3.82 us
  transfers between devices with their start and end apart: 13, of which 2 were waited for; matrix products, arithmetic and copies ran while one was open for 3% of the time, Pallas kernels for 10%

profile of v2, /device:TPU:257, one launch (start us, length us, event | category | flops | bytes accessed | tf_op | source)
XLA Modules:
  0.0 164.4 jit_solution(14814209637514855219)
XLA Ops:
  0.6 1.4 reshape.51
  2.1 1.1 copy.17
  3.2 13.5 %all-to-all-start = ((bf16[64,32,128]{2,1,0:T(8,128)(2,1)}), bf16[64,32,128]{2,1,0:T(8,128)(2,1)S(1)}, u32[]{:S(2)}, u32[]{:S(2)}) async-start(bf16[64,32,128]{2,1,0:T(8,128)(2,1)} %bitcast.44), calls=%async_computation | async-start | bytes 1048576 | tf_op jit(solution)/shard_map/all_to_all | solution.py:359
  17.6 3.1 %collective-permute-start.5 = (bf16[2048,128]{1,0:T(8,128)(2,1)}, bf16[2048,128]{1,0:T(8,128)(2,1)S(1)}, u32[]{:S(2)}, u32[]{:S(2)}) collective-permute-start(bf16[2048,128]{1,0:T(8,128)(2,1)} %pad_maximum_fusion.2), channel_id=1, source_target_pairs={{0,64},{64,128},{128,192},{192,0},{256,320},{320,384},{384,448},{4... | collective-permute-start | bytes 1572872 | tf_op jit(solution)/shard_map/ppermute | solution.py:346
  21.6 3.4 %collective-permute-start.6 = (bf16[2048,128]{1,0:T(8,128)(2,1)}, bf16[2048,128]{1,0:T(8,128)(2,1)S(1)}, u32[]{:S(2)}, u32[]{:S(2)}) collective-permute-start(bf16[2048,128]{1,0:T(8,128)(2,1)} %pad_maximum_fusion.3), channel_id=1, source_target_pairs={{0,192},{64,0},{128,64},{192,128},{256,448},{320,256},{384,320},{4... | collective-permute-start | bytes 1572872 | tf_op jit(solution)/shard_map/ppermute | solution.py:346
  25.7 4.2 %collective-permute-start.10 = (bf16[1024,128]{1,0:T(8,128)(2,1)}, bf16[1024,128]{1,0:T(8,128)(2,1)}, u32[]{:S(2)}, u32[]{:S(2)}) collective-permute-start(bf16[1024,128]{1,0:T(8,128)(2,1)} %broadcast_select_fusion), channel_id=1, source_target_pairs={{0,128},{192,64},{256,384},{448,320},{512,640},{704,576},{1,129},{... | collective-permute-start | bytes 786440 | tf_op jit(solution)/shard_map/ppermute | solution.py:346
  30.6 2.0 %collective-permute-start.2 = (bf16[1024,128]{1,0:T(8,128)(2,1)}, bf16[1024,128]{1,0:T(8,128)(2,1)}, u32[]{:S(2)}, u32[]{:S(2)}) collective-permute-start(bf16[1024,128]{1,0:T(8,128)(2,1)} %broadcast_select_fusion.2), channel_id=1, source_target_pairs={{0,64},{192,128},{256,320},{448,384},{512,576},{704,640},{1,65},{1... | collective-permute-start | bytes 786440 | tf_op jit(solution)/shard_map/ppermute | solution.py:346
  32.6 1.3 collective-permute-done.5.kv_lo
  34.0 2.4 %collective-permute-done.6.kv_hi = bf16[2048,128]{1,0:T(8,128)(2,1)S(1)} collective-permute-done((bf16[2048,128]{1,0:T(8,128)(2,1)}, bf16[2048,128]{1,0:T(8,128)(2,1)S(1)}, u32[]{:S(2)}, u32[]{:S(2)}) %collective-permute-start.6) | collective-permute-done | bytes 524320 | tf_op jit(solution)/shard_map/ppermute | solution.py:346
  36.5 5.8 %collective-permute-start.7 = (bf16[1024,128]{1,0:T(8,128)(2,1)S(1)}, bf16[1024,128]{1,0:T(8,128)(2,1)S(1)}, u32[]{:S(2)}, u32[]{:S(2)}) collective-permute-start(bf16[1024,128]{1,0:T(8,128)(2,1)S(1)} %slice_select_fusion), channel_id=1, source_target_pairs={{0,256},{256,512},{448,192},{704,448},{1,257},{257,513},{449,193},... | collective-permute-start | bytes 786440 | tf_op jit(solution)/shard_map/ppermute | solution.py:346
  43.2 2.1 %collective-permute-start = (bf16[2048,128]{1,0:T(8,128)(2,1)}, bf16[2048,128]{1,0:T(8,128)(2,1)}, u32[]{:S(2)}, u32[]{:S(2)}) collective-permute-start(bf16[2048,128]{1,0:T(8,128)(2,1)} %pad_maximum_fusion), channel_id=1, source_target_pairs={{0,64},{64,128},{128,192},{256,320},{320,384},{384,448},{512,576},... | collective-permute-start | bytes 1572872 | tf_op jit(solution)/shard_map/ppermute | solution.py:346
  45.4 1.3 collective-permute-start.1
  46.7 1.3 collective-permute-start.11
  48.0 1.3 collective-permute-start.3
  49.4 21.1 %collective-permute-start.4 = (bf16[1024,128]{1,0:T(8,128)(2,1)S(1)}, bf16[1024,128]{1,0:T(8,128)(2,1)S(1)}, u32[]{:S(2)}, u32[]{:S(2)}) collective-permute-start(bf16[1024,128]{1,0:T(8,128)(2,1)S(1)} %broadcast_select_fusion.1), channel_id=1, source_target_pairs={{192,256},{256,192},{448,512},{512,448},{193,257},{257,193},{449,5... | collective-permute-start | bytes 786440 | tf_op jit(solution)/shard_map/ppermute | solution.py:346
  71.4 6.2 %rowstats.1 = (f32[32,128]{1,0:T(8,128)}, f32[16,128]{1,0:T(8,128)}, f32[16,128]{1,0:T(8,128)}) custom-call(s32[1]{0:T(128)} %bitcast.shard, s32[768]{0:T(1024)} %reshape.48.nbr, s32[192]{0:T(256)} %cnt.5, bf16[2048,128]{1,0:T(8,128)(2,1)} %bitcast.45, bf16[2048,128]{1,0:T(8,128)(2,1)} %bitcast.51, bf16[2048,128]{1,0:T(8,128)(2,1)} %bitcast.56, ...), custom_call_target="tpu_custom_call" | custom-call | tf_op jit(solution)/shard_map/rowstats/pallas_call | solution.py:378
  77.6 1.9 %collective-permute-start.8 = (f32[16,128]{1,0:T(8,128)}, f32[16,128]{1,0:T(8,128)S(1)}, u32[]{:S(2)}, u32[]{:S(2)}) collective-permute-start(f32[16,128]{1,0:T(8,128)} %get-tuple-element.9), channel_id=1, source_target_pairs={{0,64},{64,128},{128,192},{192,256},{256,320},{320,384},{384,448},... | collective-permute-start | bytes 24584 | tf_op jit(solution)/shard_map/ppermute | solution.py:346
  79.5 9.4 %collective-permute-start.9 = (f32[16,128]{1,0:T(8,128)}, f32[16,128]{1,0:T(8,128)S(1)}, u32[]{:S(2)}, u32[]{:S(2)}) collective-permute-start(f32[16,128]{1,0:T(8,128)} %get-tuple-element.10), channel_id=1, source_target_pairs={{64,0},{128,64},{192,128},{256,192},{320,256},{384,320},{448,384},... | collective-permute-start | bytes 24584 | tf_op jit(solution)/shard_map/ppermute | solution.py:346
  88.9 9.9 %owngrads.1 = (bf16[64,32,128]{2,1,0:T(8,128)(2,1)}, f32[2048,128]{1,0:T(8,128)}, f32[2048,128]{1,0:T(8,128)}) custom-call(s32[1]{0:T(128)} %bitcast.shard, s32[768]{0:T(1024)} %reshape.48.nbr, s32[192]{0:T(256)} %cnt.5, bf16[2048,128]{1,0:T(8,128)(2,1)} %bitcast.46, bf16[2048,128]{1,0:T(8,128)(2,1)} %bitcast.52, bf16[2048,128]{1,0:T(8,128)(2,1)} %bitcast.49, ...), custom_call_target="tpu_custom_call" | custom-call | tf_op jit(solution)/shard_map/owngrads/pallas_call | solution.py:391
  99.6 7.6 %neargrads.1 = bf16[64,3,32,128]{3,2,1,0:T(8,128)(2,1)} custom-call(s32[1]{0:T(128)} %bitcast.shard, s32[768]{0:T(1024)} %reshape.48.nbr, s32[192]{0:T(256)} %cnt.5, bf16[2048,128]{1,0:T(8,128)(2,1)} %bitcast.53, bf16[2048,128]{1,0:T(8,128)(2,1)} %bitcast.50, bf16[2048,128]{1,0:T(8,128)(2,1)} %collective-permute-done.qg_lo, ...), custom_call_target="tpu_custom_call" | custom-call | tf_op jit(solution)/shard_map/neargrads/pallas_call | solution.py:405
  107.2 53.5 %all_to_all.10 = bf16[64,3,32,128]{3,2,1,0:T(8,128)(2,1)S(1)} all-to-all(bf16[64,3,32,128]{3,2,1,0:T(8,128)(2,1)} %neargrads.1), channel_id=1, replica_groups=mesh['seq'=12,'head'=64] {'head'}, dimensions={0} | all-to-all | bytes 3145728 | tf_op jit(solution)/shard_map/all_to_all | solution.py:421
  161.2 0.9 reshape.55
  162.3 0.9 reshape.56
  163.4 0.9 reshape.57
  (55 shorter events, 6.7 us)
Async XLA Ops:
  0.6 16.1 %copy-start.3 = (bf16[2048,1,128]{2,0,1:T(8,128)(2,1)S(1)}, bf16[2048,1,128]{2,0,1:T(8,128)(2,1)}, u32[]{:S(2)}) copy-start(bf16[2048,1,128]{2,0,1:T(8,128)(2,1)} %param.8) | copy-start | bytes 1572868
  2.1 14.7 %copy-start.2 = (bf16[2048,1,128]{2,0,1:T(8,128)(2,1)S(1)}, bf16[2048,1,128]{2,0,1:T(8,128)(2,1)}, u32[]{:S(2)}) copy-start(bf16[2048,1,128]{2,0,1:T(8,128)(2,1)} %param.9) | copy-start | bytes 1572868
  3.2 39.1 %all-to-all-start = ((bf16[64,32,128]{2,1,0:T(8,128)(2,1)}), bf16[64,32,128]{2,1,0:T(8,128)(2,1)S(1)}, u32[]{:S(2)}, u32[]{:S(2)}) async-start(bf16[64,32,128]{2,1,0:T(8,128)(2,1)} %bitcast.44), calls=%async_computation | async-start | bytes 1048576 | tf_op jit(solution)/shard_map/all_to_all | solution.py:359
  16.8 13.0 %copy-start = (bf16[2048,1,128]{2,0,1:T(8,128)(2,1)S(1)}, bf16[2048,1,128]{2,0,1:T(8,128)(2,1)}, u32[]{:S(2)}) copy-start(bf16[2048,1,128]{2,0,1:T(8,128)(2,1)} %param.7) | copy-start | bytes 1572868
  17.6 16.3 %collective-permute-start.5 = (bf16[2048,128]{1,0:T(8,128)(2,1)}, bf16[2048,128]{1,0:T(8,128)(2,1)S(1)}, u32[]{:S(2)}, u32[]{:S(2)}) collective-permute-start(bf16[2048,128]{1,0:T(8,128)(2,1)} %pad_maximum_fusion.2), channel_id=1, source_target_pairs={{0,64},{64,128},{128,192},{192,0},{256,320},{320,384},{384,448},{4... | collective-permute-start | bytes 1572872 | tf_op jit(solution)/shard_map/ppermute | solution.py:346
  21.6 14.8 %collective-permute-start.6 = (bf16[2048,128]{1,0:T(8,128)(2,1)}, bf16[2048,128]{1,0:T(8,128)(2,1)S(1)}, u32[]{:S(2)}, u32[]{:S(2)}) collective-permute-start(bf16[2048,128]{1,0:T(8,128)(2,1)} %pad_maximum_fusion.3), channel_id=1, source_target_pairs={{0,192},{64,0},{128,64},{192,128},{256,448},{320,256},{384,320},{4... | collective-permute-start | bytes 1572872 | tf_op jit(solution)/shard_map/ppermute | solution.py:346
  25.7 21.0 %collective-permute-start.10 = (bf16[1024,128]{1,0:T(8,128)(2,1)}, bf16[1024,128]{1,0:T(8,128)(2,1)}, u32[]{:S(2)}, u32[]{:S(2)}) collective-permute-start(bf16[1024,128]{1,0:T(8,128)(2,1)} %broadcast_select_fusion), channel_id=1, source_target_pairs={{0,128},{192,64},{256,384},{448,320},{512,640},{704,576},{1,129},{... | collective-permute-start | bytes 786440 | tf_op jit(solution)/shard_map/ppermute | solution.py:346
  30.6 17.4 %collective-permute-start.2 = (bf16[1024,128]{1,0:T(8,128)(2,1)}, bf16[1024,128]{1,0:T(8,128)(2,1)}, u32[]{:S(2)}, u32[]{:S(2)}) collective-permute-start(bf16[1024,128]{1,0:T(8,128)(2,1)} %broadcast_select_fusion.2), channel_id=1, source_target_pairs={{0,64},{192,128},{256,320},{448,384},{512,576},{704,640},{1,65},{1... | collective-permute-start | bytes 786440 | tf_op jit(solution)/shard_map/ppermute | solution.py:346
  34.0 11.4 %copy-start.4 = (bf16[2048,128]{1,0:T(8,128)(2,1)}, bf16[2048,128]{1,0:T(8,128)(2,1)S(1)}, u32[]{:S(2)}) copy-start(bf16[2048,128]{1,0:T(8,128)(2,1)S(1)} %collective-permute-done.5.kv_lo) | copy-start | bytes 1572868
  36.4 8.9 %copy-start.5 = (bf16[2048,128]{1,0:T(8,128)(2,1)}, bf16[2048,128]{1,0:T(8,128)(2,1)S(1)}, u32[]{:S(2)}) copy-start(bf16[2048,128]{1,0:T(8,128)(2,1)S(1)} %collective-permute-done.6.kv_hi) | copy-start | bytes 1572868
  36.5 12.9 %collective-permute-start.7 = (bf16[1024,128]{1,0:T(8,128)(2,1)S(1)}, bf16[1024,128]{1,0:T(8,128)(2,1)S(1)}, u32[]{:S(2)}, u32[]{:S(2)}) collective-permute-start(bf16[1024,128]{1,0:T(8,128)(2,1)S(1)} %slice_select_fusion), channel_id=1, source_target_pairs={{0,256},{256,512},{448,192},{704,448},{1,257},{257,513},{449,193},... | collective-permute-start | bytes 786440 | tf_op jit(solution)/shard_map/ppermute | solution.py:346
  42.3 3.0 %copy-start.1 = (bf16[64,32,128]{2,1,0:T(8,128)(2,1)}, bf16[64,32,128]{2,1,0:T(8,128)(2,1)S(1)}, u32[]{:S(2)}) copy-start(bf16[64,32,128]{2,1,0:T(8,128)(2,1)S(1)} %all-to-all-done) | copy-start | bytes 1572868
  42.4 28.1 %copy-start.12 = (s32[192,4]{0,1:T(4,128)S(1)}, s32[192,4]{0,1:T(4,128)}, u32[]{:S(2)}) copy-start(s32[192,4]{0,1:T(4,128)} %param.12) | copy-start | bytes 9220
  43.2 55.7 %collective-permute-start = (bf16[2048,128]{1,0:T(8,128)(2,1)}, bf16[2048,128]{1,0:T(8,128)(2,1)}, u32[]{:S(2)}, u32[]{:S(2)}) collective-permute-start(bf16[2048,128]{1,0:T(8,128)(2,1)} %pad_maximum_fusion), channel_id=1, source_target_pairs={{0,64},{64,128},{128,192},{256,320},{320,384},{384,448},{512,576},... | collective-permute-start | bytes 1572872 | tf_op jit(solution)/shard_map/ppermute | solution.py:346
  45.4 53.5 %collective-permute-start.1 = (bf16[2048,128]{1,0:T(8,128)(2,1)S(1)}, bf16[2048,128]{1,0:T(8,128)(2,1)}, u32[]{:S(2)}, u32[]{:S(2)}) collective-permute-start(bf16[2048,128]{1,0:T(8,128)(2,1)S(1)} %pad_maximum_fusion.1), channel_id=1, source_target_pairs={{64,0},{128,64},{192,128},{320,256},{384,320},{448,384},{576,512},... | collective-permute-start | bytes 1572872 | tf_op jit(solution)/shard_map/ppermute | solution.py:346
  46.7 30.9 %collective-permute-start.11 = (bf16[1024,128]{1,0:T(8,128)(2,1)}, bf16[1024,128]{1,0:T(8,128)(2,1)S(1)}, u32[]{:S(2)}, u32[]{:S(2)}) collective-permute-start(bf16[1024,128]{1,0:T(8,128)(2,1)} %collective-permute-done.10), channel_id=1, source_target_pairs={{64,256},{320,512},{384,192},{640,448},{65,257},{321,513},{385,193... | collective-permute-start | bytes 786440 | tf_op jit(solution)/shard_map/ppermute | solution.py:346
  48.0 31.5 %collective-permute-start.3 = (bf16[1024,128]{1,0:T(8,128)(2,1)}, bf16[1024,128]{1,0:T(8,128)(2,1)S(1)}, u32[]{:S(2)}, u32[]{:S(2)}) collective-permute-start(bf16[1024,128]{1,0:T(8,128)(2,1)} %collective-permute-done.2), channel_id=1, source_target_pairs={{128,256},{320,192},{384,512},{576,448},{129,257},{321,193},{385,5... | collective-permute-start | bytes 786440 | tf_op jit(solution)/shard_map/ppermute | solution.py:346
  49.4 22.0 %copy-start.6 = (bf16[1024,128]{1,0:T(8,128)(2,1)}, bf16[1024,128]{1,0:T(8,128)(2,1)S(1)}, u32[]{:S(2)}) copy-start(bf16[1024,128]{1,0:T(8,128)(2,1)S(1)} %collective-permute-done.7.kz) | copy-start | bytes 786436
  49.4 49.5 %collective-permute-start.4 = (bf16[1024,128]{1,0:T(8,128)(2,1)S(1)}, bf16[1024,128]{1,0:T(8,128)(2,1)S(1)}, u32[]{:S(2)}, u32[]{:S(2)}) collective-permute-start(bf16[1024,128]{1,0:T(8,128)(2,1)S(1)} %broadcast_select_fusion.1), channel_id=1, source_target_pairs={{192,256},{256,192},{448,512},{512,448},{193,257},{257,193},{449,5... | collective-permute-start | bytes 786440 | tf_op jit(solution)/shard_map/ppermute | solution.py:346
  77.6 11.3 %copy-start.7 = (bf16[1024,128]{1,0:T(8,128)(2,1)}, bf16[1024,128]{1,0:T(8,128)(2,1)S(1)}, u32[]{:S(2)}) copy-start(bf16[1024,128]{1,0:T(8,128)(2,1)S(1)} %collective-permute-done.11.vz) | copy-start | bytes 786436
  77.6 21.2 %collective-permute-start.8 = (f32[16,128]{1,0:T(8,128)}, f32[16,128]{1,0:T(8,128)S(1)}, u32[]{:S(2)}, u32[]{:S(2)}) collective-permute-start(f32[16,128]{1,0:T(8,128)} %get-tuple-element.9), channel_id=1, source_target_pairs={{0,64},{64,128},{128,192},{192,256},{256,320},{320,384},{384,448},... | collective-permute-start | bytes 24584 | tf_op jit(solution)/shard_map/ppermute | solution.py:346
  79.5 19.3 %copy-start.8 = (bf16[1024,128]{1,0:T(8,128)(2,1)}, bf16[1024,128]{1,0:T(8,128)(2,1)S(1)}, u32[]{:S(2)}) copy-start(bf16[1024,128]{1,0:T(8,128)(2,1)S(1)} %collective-permute-done.3.qz) | copy-start | bytes 786436
  79.5 19.3 %collective-permute-start.9 = (f32[16,128]{1,0:T(8,128)}, f32[16,128]{1,0:T(8,128)S(1)}, u32[]{:S(2)}, u32[]{:S(2)}) collective-permute-start(f32[16,128]{1,0:T(8,128)} %get-tuple-element.10), channel_id=1, source_target_pairs={{64,0},{128,64},{192,128},{256,192},{320,256},{384,320},{448,384},... | collective-permute-start | bytes 24584 | tf_op jit(solution)/shard_map/ppermute | solution.py:346
  98.9 0.7 copy-start.9
  (2 other events, 1.2 us)
